TPU v7x, 256 devices: a whole 4x4x8 slice. The times are simulated.
256 devices in a mesh: tile: 32 (over z_hi, x, core), lev: 4 (over y), sec: 2 (over z_lo).
Axes of the slice: x: 4, y: 4, z: 8 (z_hi: 4, z_lo: 2; z = z_hi * 2 + z_lo), core: 2. Of those that a mesh axis runs over, the one named last changes fastest.
Arguments:
- forcing: float32 [8, 72, 1280, 384], P('sec', 'lev', 'tile'), may hold values from -6 to 6
- courant_x: bfloat16 [72, 1280, 384], P('lev', 'tile'), may hold values from -0.44921875 to 0.44921875
- courant_y: bfloat16 [72, 1280, 384], P('lev', 'tile'), may hold values from -0.44921875 to 0.44921875
- mass_flux: bfloat16 [72, 1280, 384], P('lev', 'tile'), may hold values from 0 to 0.59765625
- limiter_code: int32 [72, 1280, 384], P('lev', 'tile'), may hold values from 0 to 15
- seam_code: int32 [32, 2], replicated, may hold values from 0 to 1
- level_weight: float32 [72], P('lev'), may hold values from 0.02 to 0.5
- sector_share: float32 [8, 1280, 384], P('sec', 'tile'), may hold values from 0.1 to 1
- flux_cell: int32 [1024, 480], P('tile'), may hold values from 0 to 15359
Outputs:
- adjoint_start: float32 [8, 72, 1280, 384], P('sec', 'lev', 'tile')
- flux_sensitivity: float32 [491520], P('tile')
All inputs are finite; a program needn't handle non-finite values.
Results may differ from a plain program's by a relative error of at most 0.0003.
Values sent between devices are 32-bit elements; how exact they have to be, the bound alone decides.
A program may use at most 128 MiB of HBM per device.

v0:
```python
import jax
import jax.numpy as jnp
from jax import lax
from jax.sharding import PartitionSpec as P

FL_DEV = 15360


def from_behind(value, axis, steps):
    count = lax.axis_size(axis)
    initial, last = (max(0, -steps), min(count, count - steps))
    return lax.ppermute(value, axis, [(source, source + steps) for source in range(initial, last)])


def extended_2(value, sides, width):
    for axis, dim in sides:
        devices, length = (lax.axis_size(axis), value.shape[dim])
        up = [(i, (i + 1) % devices) for i in range(devices)]
        down = [(j, i) for i, j in up]
        last = lax.slice_in_dim(value, length - width, length, axis=dim)
        initial = lax.slice_in_dim(value, 0, width, axis=dim)
        before = lax.ppermute(last, axis, up)
        after = lax.ppermute(initial, axis, down)
        value = jnp.concatenate([before, value, after], axis=dim)
    return value


def coefficients(courant, codes, bit):
    value = courant.astype(jnp.float32)
    limited = jnp.bitwise_and(jnp.right_shift(codes, bit), 1).astype(jnp.float32)
    spread = 0.5 * jnp.abs(value) * (1.0 - jnp.abs(value))
    ahead = jnp.maximum(value, 0.0) - limited * spread
    behind = jnp.minimum(value, 0.0) + limited * spread
    return (ahead, behind)


def flipped(rim, flag):
    return jnp.where(flag, rim[..., ::-1], rim)


def vertical(adjoint, mixing, at_top):
    above = from_behind(adjoint[:, :1], "lev", -1)
    above = jnp.where(at_top, adjoint[:, -1:], above)
    upper = jnp.concatenate([adjoint[:, 1:], above], axis=1)
    return adjoint + mixing * (upper - adjoint)


def sweep_second(adjoint, courant, codes, bit):
    ahead, behind = coefficients(courant, codes, bit)
    following = jnp.concatenate([adjoint[..., 1:], adjoint[..., -1:]], axis=-1)
    previous = jnp.concatenate([adjoint[..., :1], adjoint[..., :-1]], axis=-1)
    return adjoint + ahead * (following - adjoint) + behind * (adjoint - previous)


def sweep_first(adjoint, courant, codes, bit, flip_left, flip_right):
    ahead, behind = coefficients(courant, codes, bit)
    extended = extended_2(adjoint, (("tile", 2),), 1)
    left_rim = flipped(extended[:, :, :1], flip_left)
    right_rim = flipped(extended[:, :, -1:], flip_right)
    following = jnp.concatenate([adjoint[:, :, 1:], right_rim], axis=2)
    previous = jnp.concatenate([left_rim, adjoint[:, :, :-1]], axis=2)
    return adjoint + ahead * (following - adjoint) + behind * (adjoint - previous)


def shards(
    forcing,
    courant_x,
    courant_y,
    mass_flux,
    limiter_code,
    seam_code,
    level_weight,
    sector_share,
    flux_cell,
):
    mixing = mass_flux.astype(jnp.float32)
    at_top = lax.axis_index("lev") == lax.axis_size("lev") - 1
    tile_count = lax.axis_size("tile")
    tile_rank = lax.axis_index("tile")
    place = jnp.remainder(tile_rank + tile_count, tile_count)
    seams_here = lax.dynamic_index_in_dim(seam_code, place, 0, keepdims=False) == 1
    adjoint = forcing
    for turn_index in (1, 0):
        adjoint = vertical(adjoint, mixing, at_top)
        adjoint = sweep_second(adjoint, courant_y, limiter_code, 2 * turn_index + 1)
        adjoint = sweep_first(
            adjoint, courant_x, limiter_code, 2 * turn_index, seams_here[0], seams_here[1]
        )
    partial_value = jnp.einsum(
        "sxy,l,slxy->xy", sector_share, level_weight, adjoint, precision=lax.Precision.HIGHEST
    )
    columns = partial_value.reshape(tile_count, -1)
    totals = lax.psum(columns, ("lev", "sec"))
    received = lax.all_to_all(totals, "tile", split_axis=0, concat_axis=0, tiled=True)
    flux_sensitivity = jax.ops.segment_sum(
        received.reshape(-1), flux_cell.reshape(-1), num_segments=FL_DEV
    )
    return (adjoint, flux_sensitivity)


def solution(mesh):
    placed = (
        P("sec", "lev", "tile", None),
        P("lev", "tile", None),
        P("lev", "tile", None),
        P("lev", "tile", None),
        P("lev", "tile", None),
        P(),
        P("lev"),
        P("sec", "tile", None),
        P("tile", None),
    )
    return jax.shard_map(
        shards,
        mesh=mesh,
        in_specs=placed,
        out_specs=(P("sec", "lev", "tile", None), P("tile")),
        check_vma=False,
    )
```

profile of v0, /device:TPU:1, one launch (start us, length us, event | category | flops | bytes accessed | tf_op | source)
XLA Modules:
  0.0 220.0 jit_solution(4765529639356526114)
XLA Ops:
  1.8 1.4 collective-permute-start
  3.2 5.8 %fusion.28 = (f32[18,40,384]{2,1,0:T(8,128)}, f32[18,40,384]{2,1,0:T(8,128)}, f32[18,40,384]{2,1,0:T(8,128)}, f32[18,40,384]{2,1,0:T(8,128)}, f32[18,40,384]{2,1...) fusion(bf16[18,40,384]{2,1,0:T(8,128)(2,1)} %param.10, ...), kind=kLoop, calls=%fused_computation.45 | loop fusion | flops 10506240 | bytes 11059200 | tf_op jit(solution)/shard_map/sub | solution.py:32
  9.0 2.3 %slice.76 = f32[4,17,40,384]{3,2,1,0:T(8,128)} slice(f32[4,18,40,384]{3,2,1,0:T(8,128)S(1)} %bitcast.18), slice={[0:4], [1:18], [0:40], [0:384]} | slice | bytes 8355840 | tf_op jit(solution)/shard_map/slice | solution.py:44
  13.0 4.2 %fusion.3 = f32[4,18,40,384]{3,2,1,0:T(8,128)S(1)} fusion(f32[4,18,40,384]{3,2,1,0:T(8,128)} %param.9, f32[4,1,40,384]{3,2,1,0:T(8,128)S(1)} %slice_select_fusion.1, f32[4,17,40,384]{3,2,1,0:T(8,128)} %slice.76, f32[18,40,384]{2,1,0:T(8,128)S(1)} %convert_element_type.23), kind=kLoop, calls=%fused_computation.5 | loop fusion | flops 4423680 | bytes 14376960 | tf_op jit(solution)/shard_map/add | solution.py:45
  17.2 1.6 fusion.46
  18.8 1.4 fusion.47
  20.2 3.7 %fusion.6 = f32[4,18,40,384]{3,2,1,0:T(8,128)S(1)} fusion(f32[4,18,40,384]{3,2,1,0:T(8,128)S(1)} %fusion.3, f32[4,18,40,1]{3,2,1,0:T(8,128)} %get-tuple-element.17, f32[4,18,40,383]{3,2,1,0:T(8,128)S(1)} %get-tuple-element.19, f32[4,18,40,383]{3,2,1,0:T(8,128)S(1)} %get-tuple-element.18, f32[4,18,40,1]{3,2,1,0:T(8,128)S(1)} %get-tuple-element.16, ...), kind=kLoop, calls=%fused_computation.9 | loop fusion | flops 8847360 | bytes 19906560 | tf_op jit(solution)/shard_map/add | solution.py:52
  24.1 3.3 %collective-permute-start.1 = (f32[4,18,1,384]{3,1,2,0:T(8,128)S(1)}, f32[4,18,1,384]{3,1,2,0:T(8,128)S(1)}, u32[]{:S(2)}, u32[]{:S(2)}) collective-permute-start(f32[4,18,1,384]{3,1,2,0:T(8,128)S(1)} %copy.26), channel_id=1, source_target_pairs={{8,0},{16,8},{24,16},{32,24},{40,32},{48,40},{56,48},{64,56},{72,6... | collective-permute-start | bytes 331784 | tf_op jit(solution)/shard_map/ppermute | solution.py:23
  27.5 4.1 %fusion.45 = (f32[4,18,39,384]{3,2,1,0:T(8,128)}, f32[4,18,39,384]{3,2,1,0:T(8,128)}) fusion(f32[4,18,40,384]{3,2,1,0:T(8,128)S(1)} %fusion.6), kind=kLoop, calls=%fused_computation.74 | loop fusion | bytes 17252352 | tf_op jit(solution)/shard_map/slice | solution.py:61
  32.4 2.2 collective-permute-done.2
  37.0 5.9 %fusion.10 = f32[4,18,40,384]{3,2,1,0:T(8,128)S(1)} fusion(f32[4,18,40,384]{3,2,1,0:T(8,128)} %copy-done.2, f32[4,18,1,384]{3,2,1,0:T(1,128)S(1)} %broadcast_select_fusion.3, f32[4,18,39,384]{3,2,1,0:T(8,128)} %get-tuple-element.15, f32[4,18,39,384]{3,2,1,0:T(8,128)} %get-tuple-element.14, f32[4,18,1,384]{3,2,1,0:T(1,128)S(1)} %broadcast_select_fusion.1, ...), kind=kLoop, calls=%fused_computation.15 | loop fusion | flops 8847360 | bytes 19906560 | tf_op jit(solution)/shard_map/add | solution.py:62
  42.9 1.5 collective-permute-start.3
  44.7 5.8 %collective-permute-done.3 = f32[4,1,40,384]{3,2,1,0:T(8,128)S(1)} collective-permute-done((f32[4,1,40,384]{3,2,1,0:T(8,128)S(1)}, f32[4,1,40,384]{3,2,1,0:T(8,128)S(1)}, u32[]{:S(2)}, u32[]{:S(2)}) %collective-permute-start.3) | collective-permute-done | bytes 245792 | tf_op jit(solution)/shard_map/ppermute | solution.py:12
  51.7 1.4 fusion.43
  53.1 3.5 %fusion.16 = f32[4,18,40,384]{3,2,1,0:T(8,128)S(1)} fusion(f32[4,18,40,384]{3,2,1,0:T(8,128)S(1)} %fusion.13, f32[4,18,40,1]{3,2,1,0:T(8,128)S(1)} %get-tuple-element.9, f32[4,18,40,383]{3,2,1,0:T(8,128)S(1)} %get-tuple-element.11, f32[4,18,40,383]{3,2,1,0:T(8,128)S(1)} %get-tuple-element.10, f32[4,18,40,1]{3,2,1,0:T(8,128)S(1)} %get-tuple-element.8, ...), kind=kLoop, calls=%fused_computation.24 | loop fusion | flops 8847360 | bytes 19906560 | tf_op jit(solution)/shard_map/add | solution.py:52
  56.8 9.9 %collective-permute-start.4 = (f32[4,18,1,384]{3,1,2,0:T(8,128)S(1)}, f32[4,18,1,384]{3,1,2,0:T(8,128)S(1)}, u32[]{:S(2)}, u32[]{:S(2)}) collective-permute-start(f32[4,18,1,384]{3,1,2,0:T(8,128)S(1)} %copy.32), channel_id=1, source_target_pairs={{8,0},{16,8},{24,16},{32,24},{40,32},{48,40},{56,48},{64,56},{72,6... | collective-permute-start | bytes 331784 | tf_op jit(solution)/shard_map/ppermute | solution.py:23
  66.8 4.1 %fusion.41 = (f32[4,18,39,384]{3,2,1,0:T(8,128)}, f32[4,18,39,384]{3,2,1,0:T(8,128)}) fusion(f32[4,18,40,384]{3,2,1,0:T(8,128)S(1)} %fusion.16), kind=kLoop, calls=%fused_computation.70 | loop fusion | bytes 17252352 | tf_op jit(solution)/shard_map/slice | solution.py:61
  74.2 5.7 %fusion.20 = f32[4,18,40,384]{3,2,1,0:T(8,128)S(1)} fusion(f32[4,18,40,384]{3,2,1,0:T(8,128)} %copy-done.1, f32[4,18,1,384]{3,2,1,0:T(1,128)S(1)} %broadcast_select_fusion.2, f32[4,18,39,384]{3,2,1,0:T(8,128)} %get-tuple-element.7, f32[4,18,39,384]{3,2,1,0:T(8,128)} %get-tuple-element.6, f32[4,18,1,384]{3,2,1,0:T(1,128)S(1)} %broadcast_select_fusion, ...), kind=kLoop, calls=%fused_computation.30 | loop fusion | flops 8847360 | bytes 19906560 | tf_op jit(solution)/shard_map/add | solution.py:62
  79.9 2.1 copy-done.3
  82.0 4.4 %fusion = f32[1,4,40,384]{3,0,2,1:T(1,128)S(1)} fusion(f32[4,18,40,384]{3,2,1,0:T(8,128)S(1)} %fusion.20, f32[18]{0:T(128)S(1)} %copy-done), kind=kOutput, calls=%fused_computation.1 | convolution fusion | flops 13271040 | bytes 4669512 | tf_op jit(solution)/shard_map/sxy,l,slxy->xy/dot_general | solution.py:89
  86.5 27.3 %psum.7 = f32[32,1,480]{2,1,0:T(1,128)} all-reduce(f32[32,1,480]{2,1,0:T(1,128)S(1)} %all_to_all.6), channel_id=1, replica_groups=mesh['tile'=32,'lev'=4,'sec'=2] {'lev','sec'}, use_global_device_ids=true, to_apply=%region_0.1 | all-reduce | flops 15360 | bytes 122880 | tf_op jit(solution)/shard_map/psum | solution.py:93
  113.9 14.8 %all-to-all-start = ((f32[32,1,480]{2,1,0:T(1,128)}), f32[32,1,480]{2,1,0:T(1,128)S(1)}, u32[]{:S(2)}, u32[]{:S(2)}) async-start(f32[32,1,480]{2,1,0:T(1,128)} %psum.7), calls=%async_computation | async-start | bytes 131072 | tf_op jit(solution)/shard_map/all_to_all | solution.py:94
  128.8 9.9 %all-to-all-done = f32[32,1,480]{2,1,0:T(1,128)S(1)} async-done(((f32[32,1,480]{2,1,0:T(1,128)}), f32[32,1,480]{2,1,0:T(1,128)S(1)}, u32[]{:S(2)}, u32[]{:S(2)}) %all-to-all-start) | async-done | bytes 61472 | tf_op jit(solution)/shard_map/all_to_all | solution.py:94
  139.0 81.0 %scatter_custom_fusion = f32[15360]{0:T(1024)} fusion(s32[15360]{0:T(1024)S(1)} %reshape.33, f32[15360]{0:T(1024)S(1)} %reshape.35, f32[]{:T(128)} %constant.16.clone.1), kind=kCustom, calls=%fused_computation.65 | custom fusion | flops 15360 | bytes 61444 | tf_op jit(solution)/shard_map/scatter-add | solution.py:95
  (65 shorter events, 11.8 us)
Async XLA Ops:
  0.6 81.3 %copy-start = (f32[18]{0:T(128)S(1)}, f32[18]{0:T(128)}, u32[]{:S(2)}) copy-start(f32[18]{0:T(128)} %param.15) | copy-start | bytes 220
  0.6 8.3 %slice-start = ((s8[4423680]{0:T(1024)(128)(4,1)}), s8[4194304]{0:T(1024)(128)(4,1)S(1)}, s32[]{:S(2)}) async-start(s8[4423680]{0:T(1024)(128)(4,1)} %bitcast.17), calls=%async_computation.1 | async-start | bytes 8388608
  1.8 7.2 %slice-start.1 = ((s8[4423680]{0:T(1024)(128)(4,1)}), s8[229376]{0:T(1024)(128)(4,1)S(1)}, s32[]{:S(2)}) async-start(s8[4423680]{0:T(1024)(128)(4,1)} %bitcast.17), calls=%async_computation.2 | async-start | bytes 458752
  1.8 10.2 %collective-permute-start = (f32[4,1,40,384]{3,2,1,0:T(8,128)S(1)}, f32[4,1,40,384]{3,2,1,0:T(8,128)S(1)}, u32[]{:S(2)}, u32[]{:S(2)}) collective-permute-start(f32[4,1,40,384]{3,2,1,0:T(8,128)S(1)} %slice.78), channel_id=1, source_target_pairs={{2,0},{4,2},{6,4},{3,1},{5,3},{7,5},{10,8},{12,10},{14,12},{11,9},... | collective-permute-start | bytes 737288 | tf_op jit(solution)/shard_map/ppermute | solution.py:12
  9.0 2.3 %copy-start.7 = (bf16[18,40,384]{2,1,0:T(8,128)(2,1)S(1)}, bf16[18,40,384]{2,1,0:T(8,128)(2,1)}, u32[]{:S(2)}) copy-start(bf16[18,40,384]{2,1,0:T(8,128)(2,1)} %param.12) | copy-start | bytes 1658884
  9.0 2.4 %copy-start.10 = (s32[32,2]{0,1:T(2,128)S(1)}, s32[32,2]{0,1:T(2,128)}, u32[]{:S(2)}) copy-start(s32[32,2]{0,1:T(2,128)} %param.14) | copy-start | bytes 772
  23.9 7.7 %copy-start.2 = (f32[4,18,40,384]{3,2,1,0:T(8,128)}, f32[4,18,40,384]{3,2,1,0:T(8,128)S(1)}, u32[]{:S(2)}) copy-start(f32[4,18,40,384]{3,2,1,0:T(8,128)S(1)} %fusion.6) | copy-start | bytes 13271044
  24.1 7.5 %collective-permute-start.1 = (f32[4,18,1,384]{3,1,2,0:T(8,128)S(1)}, f32[4,18,1,384]{3,1,2,0:T(8,128)S(1)}, u32[]{:S(2)}, u32[]{:S(2)}) collective-permute-start(f32[4,18,1,384]{3,1,2,0:T(8,128)S(1)} %copy.26), channel_id=1, source_target_pairs={{8,0},{16,8},{24,16},{32,24},{40,32},{48,40},{56,48},{64,56},{72,6... | collective-permute-start | bytes 331784 | tf_op jit(solution)/shard_map/ppermute | solution.py:23
  27.4 9.6 %copy-start.6 = (f32[18,40,384]{2,1,0:T(8,128)S(1)}, f32[18,40,384]{2,1,0:T(8,128)}, u32[]{:S(2)}) copy-start(f32[18,40,384]{2,1,0:T(8,128)} %get-tuple-element.22) | copy-start | bytes 3317764
  27.4 7.1 %collective-permute-start.2 = (f32[4,18,1,384]{3,1,2,0:T(8,128)S(1)}, f32[4,18,1,384]{3,1,2,0:T(8,128)S(1)}, u32[]{:S(2)}, u32[]{:S(2)}) collective-permute-start(f32[4,18,1,384]{3,1,2,0:T(8,128)S(1)} %copy.29), channel_id=1, source_target_pairs={{0,8},{8,16},{16,24},{24,32},{32,40},{40,48},{48,56},{56,64},{64,7... | collective-permute-start | bytes 331784 | tf_op jit(solution)/shard_map/ppermute | solution.py:22
  42.9 7.6 %collective-permute-start.3 = (f32[4,1,40,384]{3,2,1,0:T(8,128)S(1)}, f32[4,1,40,384]{3,2,1,0:T(8,128)S(1)}, u32[]{:S(2)}, u32[]{:S(2)}) collective-permute-start(f32[4,1,40,384]{3,2,1,0:T(8,128)S(1)} %slice.110), channel_id=1, source_target_pairs={{2,0},{4,2},{6,4},{3,1},{5,3},{7,5},{10,8},{12,10},{14,12},{11,9},... | collective-permute-start | bytes 737288 | tf_op jit(solution)/shard_map/ppermute | solution.py:12
  56.6 14.3 %copy-start.1 = (f32[4,18,40,384]{3,2,1,0:T(8,128)}, f32[4,18,40,384]{3,2,1,0:T(8,128)S(1)}, u32[]{:S(2)}) copy-start(f32[4,18,40,384]{3,2,1,0:T(8,128)S(1)} %fusion.16) | copy-start | bytes 13271044
  56.8 14.1 %collective-permute-start.4 = (f32[4,18,1,384]{3,1,2,0:T(8,128)S(1)}, f32[4,18,1,384]{3,1,2,0:T(8,128)S(1)}, u32[]{:S(2)}, u32[]{:S(2)}) collective-permute-start(f32[4,18,1,384]{3,1,2,0:T(8,128)S(1)} %copy.32), channel_id=1, source_target_pairs={{8,0},{16,8},{24,16},{32,24},{40,32},{48,40},{56,48},{64,56},{72,6... | collective-permute-start | bytes 331784 | tf_op jit(solution)/shard_map/ppermute | solution.py:23
  66.7 7.4 %copy-start.4 = (f32[18,40,384]{2,1,0:T(8,128)S(1)}, f32[18,40,384]{2,1,0:T(8,128)}, u32[]{:S(2)}) copy-start(f32[18,40,384]{2,1,0:T(8,128)} %get-tuple-element.20) | copy-start | bytes 3317764
  66.7 7.4 %copy-start.5 = (f32[18,40,384]{2,1,0:T(8,128)S(1)}, f32[18,40,384]{2,1,0:T(8,128)}, u32[]{:S(2)}) copy-start(f32[18,40,384]{2,1,0:T(8,128)} %get-tuple-element.21) | copy-start | bytes 3317764
  66.7 5.0 %collective-permute-start.5 = (f32[4,18,1,384]{3,1,2,0:T(8,128)S(1)}, f32[4,18,1,384]{3,1,2,0:T(8,128)S(1)}, u32[]{:S(2)}, u32[]{:S(2)}) collective-permute-start(f32[4,18,1,384]{3,1,2,0:T(8,128)S(1)} %copy.35), channel_id=1, source_target_pairs={{0,8},{8,16},{16,24},{24,32},{32,40},{40,48},{48,56},{56,64},{64,7... | collective-permute-start | bytes 331784 | tf_op jit(solution)/shard_map/ppermute | solution.py:22
  79.9 2.1 copy-start.3
  82.0 4.4 %copy-start.8 = (f32[4,40,384]{2,1,0:T(8,128)S(1)}, f32[4,40,384]{2,1,0:T(8,128)}, u32[]{:S(2)}) copy-start(f32[4,40,384]{2,1,0:T(8,128)} %param.16) | copy-start | bytes 737284
  82.0 46.7 %copy-start.9 = (s32[32,480]{1,0:T(8,128)S(1)}, s32[32,480]{1,0:T(8,128)}, u32[]{:S(2)}) copy-start(s32[32,480]{1,0:T(8,128)} %param.17) | copy-start | bytes 184324
  113.9 24.8 %all-to-all-start = ((f32[32,1,480]{2,1,0:T(1,128)}), f32[32,1,480]{2,1,0:T(1,128)S(1)}, u32[]{:S(2)}, u32[]{:S(2)}) async-start(f32[32,1,480]{2,1,0:T(1,128)} %psum.7), calls=%async_computation | async-start | bytes 131072 | tf_op jit(solution)/shard_map/all_to_all | solution.py:94
where the time goes:
time: 220 us
  other arithmetic  115 us (52%)
  starting transfers between devices  31.1 us (14%)
  blocking collectives  27.3 us (12%)
  local copies, waits for them, and re-layouts  23.3 us (11%)
  waiting for transfers between devices  17.9 us (8%)
  matrix products  4.36 us (2%)
    scatter-add x1, other arithmetic, shards(): jax.ops.segment_sum(received.reshape(-1), flux_cell.reshape(-1), num_segm...  81 us
    psum x1, blocking collectives, shards(): totals = lax.psum(columns, ('lev', 'sec'))  27.3 us
    all_to_all x1, starting transfers between devices, shards(): lax.all_to_all(totals, 'tile', split_axis=0, concat_axis=0, tiled=True)  14.8 us
    ppermute x2, starting transfers between devices, extended_2(): after = lax.ppermute(initial, axis, down)  13.2 us
    add x2, other arithmetic, sweep_first(): adjoint + ahead * (following - adjoint) + behind * (adjoint - previous)  11.6 us
    all_to_all x1, waiting for transfers between devices, shards(): lax.all_to_all(totals, 'tile', split_axis=0, concat_axis=0, tiled=True)  9.88 us
    slice x2, local copies, waits for them, and re-layouts, sweep_first(): previous = jnp.concatenate([left_rim, adjoint[:, :, :-1]], axis=2)  8.13 us
    add x2, other arithmetic, sweep_second(): adjoint + ahead * (following - adjoint) + behind * (adjoint - previous)  7.2 us
  transfers between devices with their start and end apart: 7, of which 3 were waited for; matrix products, arithmetic and copies ran while one was open for 9% of the time, Pallas kernels for 0%

commit v1 on v0

--- a/solution.py
+++ b/solution.py
@@ -90,7 +90,7 @@
         "sxy,l,slxy->xy", sector_share, level_weight, adjoint, precision=lax.Precision.HIGHEST
     )
     columns = partial_value.reshape(tile_count, -1)
-    totals = lax.psum(columns, ("lev", "sec"))
+    totals = lax.psum(lax.psum(columns, "lev"), "sec")
     received = lax.all_to_all(totals, "tile", split_axis=0, concat_axis=0, tiled=True)
     flux_sensitivity = jax.ops.segment_sum(
         received.reshape(-1), flux_cell.reshape(-1), num_segments=FL_DEV

time: 220 us -> 212 us (0.964)
  blocking collectives: 27.3 us -> 20.5 us
    psum x1 -> x2, blocking collectives: 27.3 us -> 20.5 us  [shards(): totals = lax.psum(lax.psum(columns, 'lev'), 'sec')]
where the time goes in v1:
time: 212 us
  other arithmetic  115 us (54%)
  starting transfers between devices  29.7 us (14%)
  local copies, waits for them, and re-layouts  23.4 us (11%)
  blocking collectives  20.5 us (10%)
  waiting for transfers between devices  18 us (8%)
  matrix products  4.36 us (2%)
    scatter-add x1, other arithmetic, shards(): jax.ops.segment_sum(received.reshape(-1), flux_cell.reshape(-1), num_segm...  81 us
    psum x2, blocking collectives, shards(): totals = lax.psum(lax.psum(columns, 'lev'), 'sec')  20.5 us
    all_to_all x1, starting transfers between devices, shards(): lax.all_to_all(totals, 'tile', split_axis=0, concat_axis=0, tiled=True)  13.4 us
    ppermute x2, starting transfers between devices, extended_2(): after = lax.ppermute(initial, axis, down)  13.2 us
    add x2, other arithmetic, sweep_first(): adjoint + ahead * (following - adjoint) + behind * (adjoint - previous)  11.6 us
    all_to_all x1, waiting for transfers between devices, shards(): lax.all_to_all(totals, 'tile', split_axis=0, concat_axis=0, tiled=True)  9.98 us
    slice x2, local copies, waits for them, and re-layouts, sweep_first(): previous = jnp.concatenate([left_rim, adjoint[:, :, :-1]], axis=2)  8.12 us
    add x2, other arithmetic, sweep_second(): adjoint + ahead * (following - adjoint) + behind * (adjoint - previous)  7.2 us
  transfers between devices with their start and end apart: 7, of which 3 were waited for; matrix products, arithmetic and copies ran while one was open for 9% of the time, Pallas kernels for 0%

profile of v1, /device:TPU:1, one launch (start us, length us, event | category | flops | bytes accessed | tf_op | source)
XLA Modules:
  0.0 212.0 jit_solution(988451255206561793)
XLA Ops:
  1.8 1.4 collective-permute-start
  3.2 5.7 %fusion.28 = (f32[18,40,384]{2,1,0:T(8,128)}, f32[18,40,384]{2,1,0:T(8,128)}, f32[18,40,384]{2,1,0:T(8,128)}, f32[18,40,384]{2,1,0:T(8,128)}, f32[18,40,384]{2,1...) fusion(bf16[18,40,384]{2,1,0:T(8,128)(2,1)} %param.10, ...), kind=kLoop, calls=%fused_computation.45 | loop fusion | flops 10506240 | bytes 11059200 | tf_op jit(solution)/shard_map/sub | solution.py:32
  9.0 2.3 %slice.76 = f32[4,17,40,384]{3,2,1,0:T(8,128)} slice(f32[4,18,40,384]{3,2,1,0:T(8,128)S(1)} %bitcast.18), slice={[0:4], [1:18], [0:40], [0:384]} | slice | bytes 8355840 | tf_op jit(solution)/shard_map/slice | solution.py:44
  13.0 4.2 %fusion.3 = f32[4,18,40,384]{3,2,1,0:T(8,128)S(1)} fusion(f32[4,18,40,384]{3,2,1,0:T(8,128)} %param.9, f32[4,1,40,384]{3,2,1,0:T(8,128)S(1)} %slice_select_fusion.1, f32[4,17,40,384]{3,2,1,0:T(8,128)} %slice.76, f32[18,40,384]{2,1,0:T(8,128)S(1)} %convert_element_type.23), kind=kLoop, calls=%fused_computation.5 | loop fusion | flops 4423680 | bytes 14376960 | tf_op jit(solution)/shard_map/add | solution.py:45
  17.2 1.6 fusion.46
  20.2 3.7 %fusion.6 = f32[4,18,40,384]{3,2,1,0:T(8,128)S(1)} fusion(f32[4,18,40,384]{3,2,1,0:T(8,128)S(1)} %fusion.3, f32[4,18,40,1]{3,2,1,0:T(8,128)} %get-tuple-element.17, f32[4,18,40,383]{3,2,1,0:T(8,128)S(1)} %get-tuple-element.19, f32[4,18,40,383]{3,2,1,0:T(8,128)S(1)} %get-tuple-element.18, f32[4,18,40,1]{3,2,1,0:T(8,128)S(1)} %get-tuple-element.16, ...), kind=kLoop, calls=%fused_computation.9 | loop fusion | flops 8847360 | bytes 19906560 | tf_op jit(solution)/shard_map/add | solution.py:52
  24.1 3.3 %collective-permute-start.1 = (f32[4,18,1,384]{3,1,2,0:T(8,128)S(1)}, f32[4,18,1,384]{3,1,2,0:T(8,128)S(1)}, u32[]{:S(2)}, u32[]{:S(2)}) collective-permute-start(f32[4,18,1,384]{3,1,2,0:T(8,128)S(1)} %copy.26), channel_id=1, source_target_pairs={{8,0},{16,8},{24,16},{32,24},{40,32},{48,40},{56,48},{64,56},{72,6... | collective-permute-start | bytes 331784 | tf_op jit(solution)/shard_map/ppermute | solution.py:23
  27.6 4.1 %fusion.45 = (f32[4,18,39,384]{3,2,1,0:T(8,128)}, f32[4,18,39,384]{3,2,1,0:T(8,128)}) fusion(f32[4,18,40,384]{3,2,1,0:T(8,128)S(1)} %fusion.6), kind=kLoop, calls=%fused_computation.74 | loop fusion | bytes 17252352 | tf_op jit(solution)/shard_map/slice | solution.py:61
  32.5 2.2 %collective-permute-done.2 = f32[4,18,1,384]{3,1,2,0:T(8,128)S(1)} collective-permute-done((f32[4,18,1,384]{3,1,2,0:T(8,128)S(1)}, f32[4,18,1,384]{3,1,2,0:T(8,128)S(1)}, u32[]{:S(2)}, u32[]{:S(2)}) %collective-permute-start.2) | collective-permute-done | bytes 110624 | tf_op jit(solution)/shard_map/ppermute | solution.py:22
  37.1 5.9 %fusion.10 = f32[4,18,40,384]{3,2,1,0:T(8,128)S(1)} fusion(f32[4,18,40,384]{3,2,1,0:T(8,128)} %copy-done.2, f32[4,18,1,384]{3,2,1,0:T(1,128)S(1)} %broadcast_select_fusion.3, f32[4,18,39,384]{3,2,1,0:T(8,128)} %get-tuple-element.15, f32[4,18,39,384]{3,2,1,0:T(8,128)} %get-tuple-element.14, f32[4,18,1,384]{3,2,1,0:T(1,128)S(1)} %broadcast_select_fusion.1, ...), kind=kLoop, calls=%fused_computation.15 | loop fusion | flops 8847360 | bytes 19906560 | tf_op jit(solution)/shard_map/add | solution.py:62
  43.1 1.5 collective-permute-start.3
  44.8 5.8 %collective-permute-done.3 = f32[4,1,40,384]{3,2,1,0:T(8,128)S(1)} collective-permute-done((f32[4,1,40,384]{3,2,1,0:T(8,128)S(1)}, f32[4,1,40,384]{3,2,1,0:T(8,128)S(1)}, u32[]{:S(2)}, u32[]{:S(2)}) %collective-permute-start.3) | collective-permute-done | bytes 245792 | tf_op jit(solution)/shard_map/ppermute | solution.py:12
  51.8 1.4 fusion.43
  53.2 3.5 %fusion.16 = f32[4,18,40,384]{3,2,1,0:T(8,128)S(1)} fusion(f32[4,18,40,384]{3,2,1,0:T(8,128)S(1)} %fusion.13, f32[4,18,40,1]{3,2,1,0:T(8,128)S(1)} %get-tuple-element.9, f32[4,18,40,383]{3,2,1,0:T(8,128)S(1)} %get-tuple-element.11, f32[4,18,40,383]{3,2,1,0:T(8,128)S(1)} %get-tuple-element.10, f32[4,18,40,1]{3,2,1,0:T(8,128)S(1)} %get-tuple-element.8, ...), kind=kLoop, calls=%fused_computation.24 | loop fusion | flops 8847360 | bytes 19906560 | tf_op jit(solution)/shard_map/add | solution.py:52
  56.9 9.9 %collective-permute-start.4 = (f32[4,18,1,384]{3,1,2,0:T(8,128)S(1)}, f32[4,18,1,384]{3,1,2,0:T(8,128)S(1)}, u32[]{:S(2)}, u32[]{:S(2)}) collective-permute-start(f32[4,18,1,384]{3,1,2,0:T(8,128)S(1)} %copy.32), channel_id=1, source_target_pairs={{8,0},{16,8},{24,16},{32,24},{40,32},{48,40},{56,48},{64,56},{72,6... | collective-permute-start | bytes 331784 | tf_op jit(solution)/shard_map/ppermute | solution.py:23
  67.0 4.1 %fusion.41 = (f32[4,18,39,384]{3,2,1,0:T(8,128)}, f32[4,18,39,384]{3,2,1,0:T(8,128)}) fusion(f32[4,18,40,384]{3,2,1,0:T(8,128)S(1)} %fusion.16), kind=kLoop, calls=%fused_computation.70 | loop fusion | bytes 17252352 | tf_op jit(solution)/shard_map/slice | solution.py:61
  74.4 5.7 %fusion.20 = f32[4,18,40,384]{3,2,1,0:T(8,128)S(1)} fusion(f32[4,18,40,384]{3,2,1,0:T(8,128)} %copy-done.1, f32[4,18,1,384]{3,2,1,0:T(1,128)S(1)} %broadcast_select_fusion.2, f32[4,18,39,384]{3,2,1,0:T(8,128)} %get-tuple-element.7, f32[4,18,39,384]{3,2,1,0:T(8,128)} %get-tuple-element.6, f32[4,18,1,384]{3,2,1,0:T(1,128)S(1)} %broadcast_select_fusion, ...), kind=kLoop, calls=%fused_computation.30 | loop fusion | flops 8847360 | bytes 19906560 | tf_op jit(solution)/shard_map/add | solution.py:62
  80.1 2.1 copy-done.3
  82.2 4.4 %fusion = f32[1,4,40,384]{3,0,2,1:T(1,128)S(1)} fusion(f32[4,18,40,384]{3,2,1,0:T(8,128)S(1)} %fusion.20, f32[18]{0:T(128)S(1)} %copy-done), kind=kOutput, calls=%fused_computation.1 | convolution fusion | flops 13271040 | bytes 4669512 | tf_op jit(solution)/shard_map/sxy,l,slxy->xy/dot_general | solution.py:89
  86.7 13.0 %psum.14 = f32[32,480]{1,0:T(8,128)S(1)} all-reduce(f32[32,480]{1,0:T(8,128)S(1)} %reshape.28), channel_id=1, replica_groups=mesh['tile'=32,'lev'=4,'sec'=2] {'lev'}, use_global_device_ids=true, to_apply=%region_0.1 | all-reduce | flops 15360 | bytes 122880 | tf_op jit(solution)/shard_map/psum | solution.py:93
  99.8 7.5 %psum.15 = f32[32,1,480]{2,1,0:T(1,128)} all-reduce(f32[32,1,480]{2,1,0:T(1,128)S(1)} %all_to_all.6), channel_id=1, replica_groups=mesh['tile'=32,'lev'=4,'sec'=2] {'sec'}, use_global_device_ids=true, to_apply=%region_1.2 | all-reduce | flops 15360 | bytes 122880 | tf_op jit(solution)/shard_map/psum | solution.py:93
  107.2 13.4 %all-to-all-start = ((f32[32,1,480]{2,1,0:T(1,128)}), f32[32,1,480]{2,1,0:T(1,128)S(1)}, u32[]{:S(2)}, u32[]{:S(2)}) async-start(f32[32,1,480]{2,1,0:T(1,128)} %psum.15), calls=%async_computation | async-start | bytes 131072 | tf_op jit(solution)/shard_map/all_to_all | solution.py:94
  120.8 10.0 %all-to-all-done = f32[32,1,480]{2,1,0:T(1,128)S(1)} async-done(((f32[32,1,480]{2,1,0:T(1,128)}), f32[32,1,480]{2,1,0:T(1,128)S(1)}, u32[]{:S(2)}, u32[]{:S(2)}) %all-to-all-start) | async-done | bytes 61472 | tf_op jit(solution)/shard_map/all_to_all | solution.py:94
  131.0 81.0 %scatter_custom_fusion = f32[15360]{0:T(1024)} fusion(s32[15360]{0:T(1024)S(1)} %reshape.32, f32[15360]{0:T(1024)S(1)} %reshape.34, f32[]{:T(128)} %constant.16.clone.1), kind=kCustom, calls=%fused_computation.65 | custom fusion | flops 15360 | bytes 61444 | tf_op jit(solution)/shard_map/scatter-add | solution.py:95
  (67 shorter events, 13.4 us)
Async XLA Ops:
  0.6 81.5 %copy-start = (f32[18]{0:T(128)S(1)}, f32[18]{0:T(128)}, u32[]{:S(2)}) copy-start(f32[18]{0:T(128)} %param.15) | copy-start | bytes 220
  0.6 8.3 %slice-start = ((s8[4423680]{0:T(1024)(128)(4,1)}), s8[4194304]{0:T(1024)(128)(4,1)S(1)}, s32[]{:S(2)}) async-start(s8[4423680]{0:T(1024)(128)(4,1)} %bitcast.17), calls=%async_computation.1 | async-start | bytes 8388608
  1.8 7.2 %slice-start.1 = ((s8[4423680]{0:T(1024)(128)(4,1)}), s8[229376]{0:T(1024)(128)(4,1)S(1)}, s32[]{:S(2)}) async-start(s8[4423680]{0:T(1024)(128)(4,1)} %bitcast.17), calls=%async_computation.2 | async-start | bytes 458752
  1.8 10.3 %collective-permute-start = (f32[4,1,40,384]{3,2,1,0:T(8,128)S(1)}, f32[4,1,40,384]{3,2,1,0:T(8,128)S(1)}, u32[]{:S(2)}, u32[]{:S(2)}) collective-permute-start(f32[4,1,40,384]{3,2,1,0:T(8,128)S(1)} %slice.78), channel_id=1, source_target_pairs={{2,0},{4,2},{6,4},{3,1},{5,3},{7,5},{10,8},{12,10},{14,12},{11,9},... | collective-permute-start | bytes 737288 | tf_op jit(solution)/shard_map/ppermute | solution.py:12
  9.0 2.3 %copy-start.7 = (bf16[18,40,384]{2,1,0:T(8,128)(2,1)S(1)}, bf16[18,40,384]{2,1,0:T(8,128)(2,1)}, u32[]{:S(2)}) copy-start(bf16[18,40,384]{2,1,0:T(8,128)(2,1)} %param.12) | copy-start | bytes 1658884
  9.0 2.4 %copy-start.10 = (s32[32,2]{0,1:T(2,128)S(1)}, s32[32,2]{0,1:T(2,128)}, u32[]{:S(2)}) copy-start(s32[32,2]{0,1:T(2,128)} %param.14) | copy-start | bytes 772
  23.9 7.7 %copy-start.2 = (f32[4,18,40,384]{3,2,1,0:T(8,128)}, f32[4,18,40,384]{3,2,1,0:T(8,128)S(1)}, u32[]{:S(2)}) copy-start(f32[4,18,40,384]{3,2,1,0:T(8,128)S(1)} %fusion.6) | copy-start | bytes 13271044
  24.1 7.5 %collective-permute-start.1 = (f32[4,18,1,384]{3,1,2,0:T(8,128)S(1)}, f32[4,18,1,384]{3,1,2,0:T(8,128)S(1)}, u32[]{:S(2)}, u32[]{:S(2)}) collective-permute-start(f32[4,18,1,384]{3,1,2,0:T(8,128)S(1)} %copy.26), channel_id=1, source_target_pairs={{8,0},{16,8},{24,16},{32,24},{40,32},{48,40},{56,48},{64,56},{72,6... | collective-permute-start | bytes 331784 | tf_op jit(solution)/shard_map/ppermute | solution.py:23
  27.5 9.6 %copy-start.6 = (f32[18,40,384]{2,1,0:T(8,128)S(1)}, f32[18,40,384]{2,1,0:T(8,128)}, u32[]{:S(2)}) copy-start(f32[18,40,384]{2,1,0:T(8,128)} %get-tuple-element.22) | copy-start | bytes 3317764
  27.5 7.1 %collective-permute-start.2 = (f32[4,18,1,384]{3,1,2,0:T(8,128)S(1)}, f32[4,18,1,384]{3,1,2,0:T(8,128)S(1)}, u32[]{:S(2)}, u32[]{:S(2)}) collective-permute-start(f32[4,18,1,384]{3,1,2,0:T(8,128)S(1)} %copy.29), channel_id=1, source_target_pairs={{0,8},{8,16},{16,24},{24,32},{32,40},{40,48},{48,56},{56,64},{64,7... | collective-permute-start | bytes 331784 | tf_op jit(solution)/shard_map/ppermute | solution.py:22
  43.1 7.6 %collective-permute-start.3 = (f32[4,1,40,384]{3,2,1,0:T(8,128)S(1)}, f32[4,1,40,384]{3,2,1,0:T(8,128)S(1)}, u32[]{:S(2)}, u32[]{:S(2)}) collective-permute-start(f32[4,1,40,384]{3,2,1,0:T(8,128)S(1)} %slice.110), channel_id=1, source_target_pairs={{2,0},{4,2},{6,4},{3,1},{5,3},{7,5},{10,8},{12,10},{14,12},{11,9},... | collective-permute-start | bytes 737288 | tf_op jit(solution)/shard_map/ppermute | solution.py:12
  56.7 14.3 %copy-start.1 = (f32[4,18,40,384]{3,2,1,0:T(8,128)}, f32[4,18,40,384]{3,2,1,0:T(8,128)S(1)}, u32[]{:S(2)}) copy-start(f32[4,18,40,384]{3,2,1,0:T(8,128)S(1)} %fusion.16) | copy-start | bytes 13271044
  56.9 14.1 %collective-permute-start.4 = (f32[4,18,1,384]{3,1,2,0:T(8,128)S(1)}, f32[4,18,1,384]{3,1,2,0:T(8,128)S(1)}, u32[]{:S(2)}, u32[]{:S(2)}) collective-permute-start(f32[4,18,1,384]{3,1,2,0:T(8,128)S(1)} %copy.32), channel_id=1, source_target_pairs={{8,0},{16,8},{24,16},{32,24},{40,32},{48,40},{56,48},{64,56},{72,6... | collective-permute-start | bytes 331784 | tf_op jit(solution)/shard_map/ppermute | solution.py:23
  66.9 7.5 %copy-start.4 = (f32[18,40,384]{2,1,0:T(8,128)S(1)}, f32[18,40,384]{2,1,0:T(8,128)}, u32[]{:S(2)}) copy-start(f32[18,40,384]{2,1,0:T(8,128)} %get-tuple-element.20) | copy-start | bytes 3317764
  66.9 7.5 %copy-start.5 = (f32[18,40,384]{2,1,0:T(8,128)S(1)}, f32[18,40,384]{2,1,0:T(8,128)}, u32[]{:S(2)}) copy-start(f32[18,40,384]{2,1,0:T(8,128)} %get-tuple-element.21) | copy-start | bytes 3317764
  66.9 5.0 %collective-permute-start.5 = (f32[4,18,1,384]{3,1,2,0:T(8,128)S(1)}, f32[4,18,1,384]{3,1,2,0:T(8,128)S(1)}, u32[]{:S(2)}, u32[]{:S(2)}) collective-permute-start(f32[4,18,1,384]{3,1,2,0:T(8,128)S(1)} %copy.35), channel_id=1, source_target_pairs={{0,8},{8,16},{16,24},{24,32},{32,40},{40,48},{48,56},{56,64},{64,7... | collective-permute-start | bytes 331784 | tf_op jit(solution)/shard_map/ppermute | solution.py:22
  80.1 2.1 copy-start.3
  82.2 4.4 %copy-start.8 = (f32[4,40,384]{2,1,0:T(8,128)S(1)}, f32[4,40,384]{2,1,0:T(8,128)}, u32[]{:S(2)}) copy-start(f32[4,40,384]{2,1,0:T(8,128)} %param.16) | copy-start | bytes 737284
  82.2 38.5 %copy-start.9 = (s32[32,480]{1,0:T(8,128)S(1)}, s32[32,480]{1,0:T(8,128)}, u32[]{:S(2)}) copy-start(s32[32,480]{1,0:T(8,128)} %param.17) | copy-start | bytes 184324
  107.2 23.5 %all-to-all-start = ((f32[32,1,480]{2,1,0:T(1,128)}), f32[32,1,480]{2,1,0:T(1,128)S(1)}, u32[]{:S(2)}, u32[]{:S(2)}) async-start(f32[32,1,480]{2,1,0:T(1,128)} %psum.15), calls=%async_computation | async-start | bytes 131072 | tf_op jit(solution)/shard_map/all_to_all | solution.py:94
